TPU v7x, 512 devices: a whole 4x8x8 slice. The times are simulated.
512 devices in a mesh: ens: 32 (over x_hi, z, core), tile: 16 (over x_lo, y).
Axes of the slice: x: 4 (x_hi: 2, x_lo: 2; x = x_hi * 2 + x_lo), y: 8, z: 8, core: 2. Of those that a mesh axis runs over, the one named last changes fastest.
Arguments:
- coords: float32 [256, 3, 3200], P('ens', None, 'tile'), may hold values from -6 to 6
- counts: int32 [3200, 3200], P('tile'), may hold values from 0 to 63, as said below
- segments: int32 [3200], replicated, may hold values from 0 to 7, never falling along the last dimension, each value on 1 to 800 neighbouring positions
Outputs:
- gradient: float32 [256, 3, 3200], P('ens', None, 'tile')
Inputs may be any that keep to these rules, and one draw needn't show every extreme that they name: counts is symmetric: counts[i, j] == counts[j, i].
All inputs are finite; a program needn't handle non-finite values.
Results may differ from a plain program's by a relative error of at most 0.00011.
Values sent between devices are 32-bit elements; how exact they have to be, the bound alone decides.
A program may use at most 64 MiB of HBM per device.

v0:
```python
import jax
import jax.numpy as jnp
from jax import lax
from jax.sharding import PartitionSpec as P


def pair_sigmoid(rows_xyz, all_xyz):
    gap = rows_xyz[:, :, None] - all_xyz[:, None, :]
    dist = jnp.sum(gap * gap, axis=0)
    return jax.nn.sigmoid(1.0 * (6.0 - dist))


def on_device(coords, counts, segments):
    local_n = coords.shape[0]
    bead_rows = coords.shape[2]
    n_tile = lax.axis_size("tile")
    n_ens = lax.axis_size("ens")
    beads = bead_rows * n_tile
    structs = local_n * n_ens
    tile_pos = lax.axis_index("tile")
    all_coords = lax.all_gather(coords, "tile", axis=2, tiled=True)
    row_start = tile_pos * bead_rows
    seg_rows = lax.dynamic_slice_in_dim(segments, row_start, bead_rows)
    count_f = counts.astype(jnp.float32)
    target = count_f / (count_f + 8.0)
    row_ids = row_start + lax.broadcasted_iota(jnp.int32, (bead_rows, beads), 0)
    col_ids = lax.broadcasted_iota(jnp.int32, (bead_rows, beads), 1)
    same = seg_rows[:, None] == segments[None, :]
    weight = jnp.where(row_ids == col_ids, 0.0, jnp.where(same, 1.0, 0.3)).astype(jnp.float32)

    def accumulate(total, pair):
        return (total + pair_sigmoid(pair[0], pair[1]), None)

    total, unused = lax.scan(
        accumulate, jnp.zeros((bead_rows, beads), jnp.float32), (coords, all_coords)
    )
    pbar = lax.psum(total, "ens") / structs
    weighted = weight * (pbar - target)

    def pair_terms(pair):
        rows_xyz, all_xyz = pair
        sig = pair_sigmoid(rows_xyz, all_xyz)
        term = weighted * sig * (1.0 - sig)
        rowsum = jnp.sum(term, axis=1)
        mixed = jnp.einsum(
            "cj,ij->ci",
            all_xyz,
            term,
            precision=lax.Precision.HIGHEST,
            preferred_element_type=jnp.float32,
        )
        return (term, rowsum, mixed)

    def half_grads(pair):
        rows_xyz, all_xyz = pair
        term, rowsum, mixed = pair_terms(pair)
        own_part = -(1.0 / 32) * (rowsum[None, :] * rows_xyz - mixed)
        colsum = jnp.sum(term, axis=0)
        crossed = jnp.einsum(
            "ci,ij->cj",
            rows_xyz,
            term,
            precision=lax.Precision.HIGHEST,
            preferred_element_type=jnp.float32,
        )
        other_part = -(1.0 / 32) * (colsum[None, :] * all_xyz - crossed)
        return (own_part, other_part)

    own_parts, other_parts = lax.map(half_grads, (coords, all_coords))
    received = lax.psum_scatter(other_parts, "tile", scatter_dimension=2, tiled=True)
    return own_parts + received


def solution(mesh):
    return jax.shard_map(
        on_device,
        mesh=mesh,
        in_specs=(P("ens", None, "tile"), P("tile", None), P()),
        out_specs=P("ens", None, "tile"),
        check_vma=False,
    )
```

profile of v0, /device:TPU:1, one launch (start us, length us, event | category | flops | bytes accessed | tf_op | source)
XLA Modules:
  0.0 609.9 jit_solution(11675513955318887632)
XLA Ops:
  8.2 78.5 %all_gather.3 = f32[8,3,3200]{0,1,2:T(4,128)} all-gather(f32[8,3,200]{0,1,2:T(4,128)S(1)} %copy.20), channel_id=1, replica_groups=mesh['ens'=32,'tile'=16] {'tile'}, dimensions={2}, use_global_device_ids=true | all-gather | bytes 326400 | tf_op jit(solution)/shard_map/all_gather | solution.py:21
  86.8 5.1 copy.24
  91.9 37.9 %while.24 = (s32[]{:T(128)}, f32[200,3200]{1,0:T(8,128)}, f32[8,3,200]{2,1,0:T(4,128)S(1)}, f32[8,3,3200]{2,1,0:T(4,128)S(1)}, s32[]{:T(128)}, /*index=5*/s32[]{:T(128)}) while((s32[]{:T(128)}, f32[200,3200]{1,0:T(8,128)}, f32[8,3,200]{2,1,0:T(4,128)S(1)}, f32[8,3,3200]{2,1,0:T(4,128)S(1)}, s32[]{:T(128)}, ...), condition=%wide.region_2.3_spmd.clone, body=%wide.region_0.2_spmd.clone.sunk | while | flops 8960003 | bytes 10362487 | solution.py:34
  92.9 2.2 select_add_fusion.2
  96.1 3.9 select_add_fusion.2
  101.1 3.9 select_add_fusion.2
  106.0 3.9 select_add_fusion.2
  110.9 3.9 select_add_fusion.2
  115.9 3.9 select_add_fusion.2
  120.8 3.9 select_add_fusion.2
  125.8 3.9 select_add_fusion.2
  130.5 285.7 %all-reduce.4.cloned.1.call-done = f32[200,3200]{1,0:T(8,128)} async-done(((f32[200,3200]{1,0:T(8,128)}), f32[200,3200]{1,0:T(8,128)}) %all-reduce.4.cloned.1.call-update) | async-done | bytes 2560016 | tf_op jit(solution)/shard_map/psum | solution.py:37
  416.2 4.3 fusion.5
  420.4 53.8 %while.23 = (s32[]{:T(128)}, f32[8,3,200]{2,0,1:T(8,128)S(1)}, f32[8,3,3200]{2,0,1:T(8,128)S(1)}, f32[8,3,200]{2,1,0:T(4,128)S(1)}, f32[8,3,3200]{2,1,0:T(4,128)...) while((s32[]{:T(128)}, f32[8,3,200]{2,0,1:T(8,128)S(1)}, f32[8,3,3200]{2,0,1:T(8,128)S(1)}, ...), condition=%wide.region_8.9_spmd, body=%wide.region_4.8_spmd.sunk | while | flops 56987200 | bytes 26035328 | solution.py:69
  423.3 1.3 fusion.24
  424.9 2.2 fusion.23
  430.0 1.3 fusion.24
  431.6 2.2 fusion.23
  436.8 1.3 fusion.24
  438.3 2.2 fusion.23
  443.5 1.3 fusion.24
  445.1 2.2 fusion.23
  450.2 1.3 fusion.24
  451.8 2.2 fusion.23
  457.0 1.3 fusion.24
  458.5 2.2 fusion.23
  463.7 1.3 fusion.24
  465.3 2.2 fusion.23
  470.4 1.3 fusion.24
  472.0 2.2 fusion.23
  476.9 124.7 %all-reduce.6.cloned.1.call-done = f32[8,3,3200]{2,0,1:T(8,128)} async-done(((f32[8,3,3200]{2,0,1:T(8,128)}), f32[8,3,3200]{2,0,1:T(8,128)}) %all-reduce.6.cloned.1.call-update) | async-done | bytes 307216
  601.6 1.5 dynamic-slice_add_fusion
  (122 shorter events, 37.5 us)
Async XLA Ops:
  6.5 409.6 %all-reduce.4.cloned.1.call-start = ((), (), s32[]{:S(2)}) async-start(), calls=%async_computation | async-start | bytes 5120000 | tf_op jit(solution)/shard_map/psum | solution.py:37
  129.7 0.7 copy-start.3
  129.7 286.5 %copy-start.1 = (s32[200,3200]{1,0:T(8,128)S(1)}, s32[200,3200]{1,0:T(8,128)}, u32[]{:S(2)}) copy-start(s32[200,3200]{1,0:T(8,128)} %param.8) | copy-start | bytes 7680004
  129.8 471.8 %all-reduce.6.cloned.1.call-start = ((), (), s32[]{:S(2)}) async-start(), calls=%async_computation.1 | async-start | bytes 614400
  420.4 1.7 copy-start
  427.2 1.7 copy-start
  433.9 1.7 copy-start
  440.6 1.7 copy-start
  447.3 1.7 copy-start
  454.1 1.7 copy-start
  460.8 1.7 copy-start
  467.5 1.7 copy-start
  474.2 0.7 copy-start.2
Sparse Core Ops, SparseCore 0:
  129.9 286.2 all-reduce.3
  475.1 126.4 all-reduce.5
where the time goes:
time: 620 us; the launch traced here: 610 us
  waiting for transfers between devices  410 us (66%)
  blocking collectives  78.5 us (13%)
  other arithmetic  60.1 us (10%)
  matrix products  27.9 us (4%)
  local copies, waits for them, and re-layouts  18 us (3%)
  between operations  14.1 us (2%)
    psum x1, waiting for transfers between devices, on_device(): pbar = lax.psum(total, 'ens') / structs  286 us
    unnamed x3, waiting for transfers between devices  125 us
    all_gather x1, blocking collectives, on_device(): all_coords = lax.all_gather(coords, 'tile', axis=2, tiled=True)  78.5 us
    add x8, other arithmetic, accumulate(): return (total + pair_sigmoid(pair[0], pair[1]), None)  29.8 us
    dot_general x8, matrix products, pair_terms(): jnp.einsum('cj,ij->ci', all_xyz, term, precision=lax.Precision.HIGHEST, p...  17.3 us
    reduce_sum x16, other arithmetic, pair_sigmoid(): dist = jnp.sum(gap * gap, axis=0)  15.3 us
  transfers between devices with their start and end apart: 2, of which 2 were waited for; matrix products, arithmetic and copies ran while one was open for 0% of the time, Pallas kernels for 0%

commit v1 on v0

v1 whole, which is shorter than its diff:
```python
import functools

import jax
import jax.numpy as jnp
from jax import lax
from jax.experimental import pallas as pl
from jax.experimental.pallas import tpu as pltpu
from jax.sharding import PartitionSpec as P

MESH = pl.DeviceIdType.MESH
LANES = 128
WINDOW = 384
F32 = jnp.float32


def up(n, m):
    return (n + m - 1) // m * m


def partner_order(n):
    half = n // 2
    pairs = [(a, b) for a in range(2) for b in range(half) if (a, b) != (0, 0)]
    return sorted(pairs, key=lambda p: p[0] + min(p[1], half - p[1]))


def member(index, offset, n):
    a, b = offset
    half = n // 2
    return lax.rem(lax.div(index, half) + a, 2) * half + lax.rem(lax.rem(index, half) + b, half)


def against(a, b):
    return lax.dot_general(a, b, (((1,), (1,)), ((), ())), preferred_element_type=F32)


def kernel(
    n, structs, coords_ref, counts_ref, seg_ref, out_ref,
    mine, tiles, rows_in, cols_in, row_t, col_t, row_c, col_c, tanhs,
    window, rest, scale, weights, part, other, grad_t, grad_s, parts_in,
    tile_send, tile_recv, row_send, row_recv, col_send, col_recv, core_send, core_recv,
    out_send, out_recv, count_sem,
):
    _, local_n, rows = coords_ref.shape
    beads = counts_ref.shape[1]
    width = mine.shape[1]
    lanes = n * local_n
    second = rows - LANES
    halves = ((0, LANES), (LANES, second))
    cuts = (0, 3 * LANES, grad_s.shape[2])
    order = partner_order(n)
    ens = lax.axis_index("ens")
    t = lax.axis_index("tile")
    me, core = lax.div(ens, 2), lax.rem(ens, 2)

    def window_of(tile):
        first = tile * rows
        start = jnp.minimum(lax.div(first, LANES) * LANES, beads - WINDOW)
        return pl.multiple_of(start, LANES), first - start

    col_start, col_off = window_of(me)
    row_start, row_off = window_of(t)
    counts_copy = pltpu.make_async_copy(counts_ref.at[:, pl.ds(col_start, WINDOW)], window, count_sem)
    counts_copy.start()

    barrier = pltpu.get_barrier_semaphore()
    for offset in order:
        pl.semaphore_signal(barrier, inc=1, device_id={"tile": member(t, offset, n)}, device_id_type=MESH)
        pl.semaphore_signal(
            barrier, inc=1, device_id={"ens": member(me, offset, n) * 2 + core}, device_id_type=MESH
        )
    pl.semaphore_signal(barrier, inc=1, device_id={"ens": me * 2 + 1 - core}, device_id_type=MESH)

    for c in range(3):
        mine[:, c * rows : (c + 1) * rows] = coords_ref[c]
    mine[:, 3 * rows :] = jnp.zeros((local_n, width - 3 * rows), F32)
    part[...] = jnp.zeros_like(part)
    rows_in[me] = mine[...]

    pl.semaphore_wait(barrier, 2 * len(order) + 1)

    def to_tile(offset):
        p = member(t, offset, n)
        return pltpu.make_async_remote_copy(
            mine, tiles.at[t], tile_send.at[p], tile_recv.at[t], device_id={"tile": p}, device_id_type=MESH
        )

    def from_tile(p):
        return pltpu.make_async_remote_copy(
            mine, tiles.at[p], tile_send.at[p], tile_recv.at[p], device_id={"tile": p}, device_id_type=MESH
        )

    def to_row(offset):
        p = member(me, offset, n)
        return pltpu.make_async_remote_copy(
            mine, rows_in.at[me], row_send.at[p], row_recv.at[me],
            device_id={"ens": p * 2 + core}, device_id_type=MESH,
        )

    def from_row(p):
        return pltpu.make_async_remote_copy(
            mine, rows_in.at[p], row_send.at[p], row_recv.at[p],
            device_id={"ens": p * 2 + core}, device_id_type=MESH,
        )

    def to_col(source, p):
        return pltpu.make_async_remote_copy(
            source, cols_in.at[me], col_send.at[p], col_recv.at[me],
            device_id={"ens": p * 2 + core}, device_id_type=MESH,
        )

    def from_col(p):
        return pltpu.make_async_remote_copy(
            mine, cols_in.at[p], col_send.at[p], col_recv.at[p],
            device_id={"ens": p * 2 + core}, device_id_type=MESH,
        )

    for offset in order:
        to_tile(offset).start()

    @pl.when(t != me)
    def _():
        to_col(mine, t).start()

    for offset in order:
        to_row(offset).start()

    counts_copy.wait()
    lane_ids = lax.broadcasted_iota(jnp.int32, (rows, WINDOW), 1)
    bead_ids = lax.broadcasted_iota(jnp.int32, (rows, WINDOW), 0)
    pick_col = lane_ids == bead_ids + col_off
    pick_row = (lane_ids == bead_ids + row_off).astype(F32).astype(jnp.bfloat16)
    seg_col = jnp.sum(
        jnp.where(pick_col, seg_ref[:, pl.ds(col_start, WINDOW)].astype(F32), 0.0), axis=1, keepdims=True
    )
    seg_rows = jnp.broadcast_to(
        seg_ref[:, pl.ds(row_start, WINDOW)].astype(F32), (8, WINDOW)
    ).astype(jnp.bfloat16)
    pick_col = pick_col.astype(F32).astype(jnp.bfloat16)
    for h, (first, size) in enumerate(halves):
        counts_f = window[first : first + size, :].astype(F32).astype(jnp.bfloat16)
        count = against(pick_col, counts_f)
        seg_row = against(seg_rows, pick_row[first : first + size, :])[0:1, :]
        same = seg_col == seg_row
        diagonal = (
            me * rows + lax.broadcasted_iota(jnp.int32, (rows, size), 0)
            == t * rows + first + lax.broadcasted_iota(jnp.int32, (rows, size), 1)
        )
        weight = jnp.where(diagonal, 0.0, jnp.where(same, 1.0, 0.3))
        rest[h, :, 0:size] = 0.5 - count / (count + 8.0)
        scale[h, :, 0:size] = weight * (-1.0 / 64.0)
        if size < LANES:
            rest[h, :, size:] = jnp.zeros((rows, LANES - size), F32)
            scale[h, :, size:] = jnp.zeros((rows, LANES - size), F32)

    for offset in order:
        p = member(t, offset, n)
        from_tile(p).wait_recv()

        @pl.when(p != me)
        def _():
            to_col(tiles.at[p], p).start()

        @pl.when(p == me)
        def _():
            cols_in[me] = tiles[me]

    @pl.when(t == me)
    def _():
        cols_in[me] = mine[...]

    def turn(source, target):
        for b in range(width // LANES):
            block = source[:, :, b * LANES : (b + 1) * LANES].reshape(lanes, LANES)
            target[b * LANES : (b + 1) * LANES, :] = block.T

    def norms(target, bias):
        x, y, z = (target[c * rows : (c + 1) * rows, :] for c in range(3))
        return bias - 0.5 * (x * x + y * y + z * z)

    for offset in order:
        from_row(member(me, offset, n)).wait_recv()
    turn(rows_in, row_t)
    row_c[...] = norms(row_t, 3.0)

    for offset in order:
        from_col(member(me, offset, n)).wait_recv()
    turn(cols_in, col_t)
    col_c[...] = norms(col_t, 0.0)

    blocks = rows // 8
    lane = lax.broadcasted_iota(jnp.int32, (8, LANES), 1)

    def col_block(j):
        return [col_t[pl.ds(pl.multiple_of(c * rows + 8 * j, 8), 8), :] for c in range(3)]

    def row_of(ref, r):
        return jnp.broadcast_to(ref[pl.ds(r, 1), :], (8, lanes))

    def sigmoids(h):
        first, size = halves[h]

        def row_block(b, carry):
            i = first + 8 * b
            at = [[row_of(row_t, c * rows + i + q) for c in range(3)] for q in range(8)]
            bias = [row_of(row_c, i + q) for q in range(8)]

            def pairs(j, carry):
                x, y, z = col_block(j)
                own = pl.ds(pl.multiple_of(8 * j, 8), 8)
                cj = col_c[own, :]
                total = part[h, own, :]
                for q in range(8):
                    xi, yi, zi = at[q]
                    v = jnp.tanh(((bias[q] + cj) + xi * x) + (yi * y + zi * z))
                    tanhs[first // 8 + b, j, q] = v
                    total = jnp.where(lane == 8 * b + q, jnp.sum(v, axis=1, keepdims=True), total)
                part[h, own, :] = total
                return carry

            return lax.fori_loop(0, blocks, pairs, carry, unroll=25)

        lax.fori_loop(0, size // 8, row_block, 0)

    def swap(h):
        return pltpu.make_async_remote_copy(
            part.at[h], other.at[h], core_send.at[h], core_recv.at[h],
            device_id={"ens": me * 2 + 1 - core}, device_id_type=MESH,
        )

    def gradients(h):
        first, size = halves[h]
        pitch = LANES if h == 0 else second

        def row_block(b, carry):
            i = first + 8 * b
            down = [[], [], []]
            for group in range(0, 8, 2):
                members = range(group, group + 2)

                def pairs(j, sums):
                    x, y, z = col_block(j)
                    w = weights[h, pl.ds(pl.multiple_of(8 * j, 8), 8), :]
                    w = pltpu.roll(w, lax.rem(LANES - 8 * b, LANES), 1)
                    new = []
                    for q, (s, sx, sy, sz) in zip(members, sums):
                        v = tanhs[first // 8 + b, j, q]
                        wq = jnp.broadcast_to(w[:, q : q + 1], (8, lanes))
                        g = wq - wq * (v * v)
                        new.append((s + g, sx + g * x, sy + g * y, sz + g * z))
                    return tuple(new)

                zero = jnp.zeros((8, lanes), F32)
                sums = lax.fori_loop(0, blocks, pairs, ((zero,) * 4,) * 2, unroll=25)
                for c in range(3):
                    for q, total in zip(members, sums):
                        down[c].append(
                            jnp.sum(row_of(row_t, c * rows + i + q) * total[0] - total[c + 1], axis=0, keepdims=True)
                        )
            for c in range(3):
                at = pl.multiple_of(cuts[h] + c * pitch + 8 * b, 8)
                grad_t[pl.ds(at, 8), :] = jnp.concatenate(down[c], axis=0)
            return carry

        lax.fori_loop(0, size // 8, row_block, 0)

    def to_owner(h, p):
        cut = slice(cuts[h], cuts[h + 1])
        return pltpu.make_async_remote_copy(
            grad_s.at[p, :, cut], parts_in.at[me, :, cut], out_send.at[h, p], out_recv.at[h, me],
            device_id={"ens": p * 2 + core}, device_id_type=MESH,
        )

    def from_sharer(h, p):
        cut = slice(cuts[h], cuts[h + 1])
        return pltpu.make_async_remote_copy(
            grad_s.at[p, :, cut], parts_in.at[p, :, cut], out_send.at[h, p], out_recv.at[h, p],
            device_id={"ens": p * 2 + core}, device_id_type=MESH,
        )

    for h in range(2):
        sigmoids(h)
        swap(h).start()
    used = cuts[1] + 3 * second
    grad_t[used:, :] = jnp.zeros((grad_t.shape[0] - used, lanes), F32)
    for h in range(2):
        swap(h).wait()
        mean = (part[h] + other[h]) * (1.0 / structs) * 0.5
        weights[h] = scale[h] * (rest[h] + mean)
        gradients(h)
        for b in range(cuts[h] // LANES, cuts[h + 1] // LANES):
            block = grad_t[b * LANES : (b + 1) * LANES, :].T
            grad_s[:, :, b * LANES : (b + 1) * LANES] = block.reshape(n, local_n, LANES)
        for offset in reversed(order):
            to_owner(h, member(me, offset, n)).start()

    for h, (first, size) in enumerate(halves):
        pitch = LANES if h == 0 else second
        total = grad_s[me, :, cuts[h] : cuts[h + 1]]
        for offset in order:
            p = member(me, offset, n)
            from_sharer(h, p).wait_recv()
            total = total + parts_in[p, :, cuts[h] : cuts[h + 1]]
        for c in range(3):
            out_ref[c, :, first : first + size] = total[:, c * pitch : c * pitch + size]

    for offset in order:
        to_tile(offset).wait_send()
        to_row(offset).wait_send()
        p = member(me, offset, n)
        for h in range(2):
            to_owner(h, p).wait_send()
        to_col(mine, p).wait_send()


def solution(mesh):
    n = mesh.shape["tile"]

    def on_device(coords, counts, segments):
        local_n, _, rows = coords.shape
        structs = local_n * mesh.shape["ens"]
        lanes = n * local_n
        width = up(3 * rows, LANES)
        wide = 3 * LANES + up(3 * (rows - LANES), LANES)
        blocks = rows // 8
        vmem, dma = pltpu.VMEM, pltpu.SemaphoreType.DMA
        out = pl.pallas_call(
            functools.partial(kernel, n, structs),
            out_shape=jax.ShapeDtypeStruct((3, local_n, rows), F32),
            in_specs=[
                pl.BlockSpec(memory_space=pltpu.VMEM),
                pl.BlockSpec(memory_space=pl.ANY),
                pl.BlockSpec(memory_space=pltpu.VMEM),
            ],
            out_specs=pl.BlockSpec(memory_space=pltpu.VMEM),
            scratch_shapes=[
                vmem((local_n, width), F32),
                vmem((n, local_n, width), F32),
                vmem((n, local_n, width), F32),
                vmem((n, local_n, width), F32),
                vmem((width, lanes), F32),
                vmem((width, lanes), F32),
                vmem((rows, lanes), F32),
                vmem((rows, lanes), F32),
                vmem((blocks, blocks, 8, 8, lanes), F32),
                vmem((rows, WINDOW), jnp.int32),
                vmem((2, rows, LANES), F32),
                vmem((2, rows, LANES), F32),
                vmem((2, rows, LANES), F32),
                vmem((2, rows, LANES), F32),
                vmem((2, rows, LANES), F32),
                vmem((wide, lanes), F32),
                vmem((n, local_n, wide), F32),
                vmem((n, local_n, wide), F32),
                dma((n,)), dma((n,)), dma((n,)), dma((n,)), dma((n,)), dma((n,)),
                dma((2,)), dma((2,)), dma((2, n)), dma((2, n)), dma,
            ],
            compiler_params=pltpu.CompilerParams(
                collective_id=0, has_side_effects=True, vmem_limit_bytes=60 * 1024 * 1024
            ),
        )(coords.transpose(1, 0, 2), counts, segments.reshape(1, -1))
        return out.transpose(1, 0, 2)

    return jax.shard_map(
        on_device,
        mesh=mesh,
        in_specs=(P("ens", None, "tile"), P("tile", None), P()),
        out_specs=P("ens", None, "tile"),
        check_vma=False,
    )
```

time: 620 us -> 72.6 us (0.12)
  the two profiles are of different devices: /device:TPU:1 before, /device:TPU:24 now
where the time goes in v1:
time: 72.6 us; the launch traced here: 72.3 us
  Pallas kernels  69.6 us (96%)
  local copies, waits for them, and re-layouts  2.67 us (4%)
    pallas_call x1, Pallas kernels, on_device(): pl.pallas_call(functools.partial(kernel, n, structs), out_shape=jax.Shape...  69.6 us

profile of v1, /device:TPU:24, one launch (start us, length us, event | category | flops | bytes accessed | tf_op | source)
XLA Modules:
  0.0 72.3 jit_solution(13129235579789352045)
XLA Ops:
  0.0 1.3 %reshape.3.seg_ref = s32[1,3200]{1,0:T(1,128)} reshape(s32[3200]{0:T(1024)} %param.5) | data formatting | bytes 25600 | tf_op jit(solution)/shard_map/reshape | solution.py:360
  1.3 69.6 %shard_map.37 = f32[3,8,200]{2,1,0:T(8,128)} custom-call(f32[3,8,200]{2,1,0:T(8,128)} %bitcast.3, s32[200,3200]{1,0:T(8,128)} %counts_ref.1, s32[1,3200]{1,0:T(1,128)} %reshape.3.seg_ref), custom_call_target="tpu_custom_call" | custom-call | tf_op jit(solution)/shard_map/pallas_call | solution.py:326
  71.0 1.3 %copy.5 = f32[8,3,200]{2,0,1:T(8,128)} copy(f32[8,3,200]{2,0,1:T(8,128)} %bitcast.2) | data formatting | bytes 38400

commit v2 on v0

v2 whole, which is shorter than its diff:
```python
import functools

import jax
import jax.numpy as jnp
from jax import lax
from jax.experimental import pallas as pl
from jax.experimental.pallas import tpu as pltpu
from jax.sharding import PartitionSpec as P

MESH = pl.DeviceIdType.MESH
LANES = 128
WINDOW = 384
GROUP = 5
CHUNK = 8 * GROUP
F32 = jnp.float32


def up(n, m):
    return (n + m - 1) // m * m


def partner_order(n):
    half = n // 2
    pairs = [(a, b) for a in range(2) for b in range(half) if (a, b) != (0, 0)]
    return sorted(pairs, key=lambda p: p[0] + min(p[1], half - p[1]))


def member(index, offset, n):
    a, b = offset
    half = n // 2
    return lax.rem(lax.div(index, half) + a, 2) * half + lax.rem(lax.rem(index, half) + b, half)


def against(a, b):
    return lax.dot_general(a, b, (((1,), (1,)), ((), ())), preferred_element_type=F32)


def kernel(
    n, structs, coords_ref, counts_ref, seg_ref, out_ref,
    mine, tiles, rows_in, cols_in, row_t, col_t, row_c, col_c, tanhs,
    window, rest, scale, weights, part, other, grad_t, grad_s, parts_in,
    tile_send, tile_pass, tile_recv, row_send, row_pass, row_recv, col_send, col_recv, core_send, core_recv,
    out_send, out_recv, count_sem,
):
    _, local_n, rows = coords_ref.shape
    beads = counts_ref.shape[1]
    lanes = n * local_n
    blocks = rows // 8
    chunks = rows // CHUNK
    order = partner_order(n)
    line = [offset for offset in order if offset[0] == 0]
    over = [offset for offset in order if offset[0] == 1]
    near = line + over[:1]
    split = max(1, 2 * chunks // 5)
    parts = ((0, split), (split, chunks))
    ens = lax.axis_index("ens")
    t = lax.axis_index("tile")
    me, core = lax.div(ens, 2), lax.rem(ens, 2)

    def window_of(tile):
        first = tile * rows
        start = jnp.minimum(lax.div(first, LANES) * LANES, beads - WINDOW)
        return pl.multiple_of(start, LANES), first - start

    col_start, col_off = window_of(me)
    row_start, row_off = window_of(t)
    counts_copy = pltpu.make_async_copy(counts_ref.at[:, pl.ds(col_start, WINDOW)], window, count_sem)
    counts_copy.start()

    barrier = pltpu.get_barrier_semaphore()
    for offset in near:
        pl.semaphore_signal(barrier, inc=1, device_id={"tile": member(t, offset, n)}, device_id_type=MESH)
    for offset in order:
        pl.semaphore_signal(
            barrier, inc=1, device_id={"ens": member(me, offset, n) * 2 + core}, device_id_type=MESH
        )
    pl.semaphore_signal(barrier, inc=1, device_id={"ens": me * 2 + 1 - core}, device_id_type=MESH)

    for h in range(chunks):
        for c in range(3):
            mine[h, :, c * CHUNK : (c + 1) * CHUNK] = coords_ref[c, :, h * CHUNK : (h + 1) * CHUNK]
        mine[h, :, 3 * CHUNK :] = jnp.zeros((local_n, LANES - 3 * CHUNK), F32)
    rows_in[me] = mine[...]

    pl.semaphore_wait(barrier, len(near) + len(order) + 1)

    def of(part):
        return slice(parts[part][0], parts[part][1])

    def tile_copy(a, source, sem, p, slot):
        return pltpu.make_async_remote_copy(
            source.at[of(a)], tiles.at[slot, of(a)], sem, tile_recv.at[a, slot],
            device_id={"tile": p}, device_id_type=MESH,
        )

    def row_copy(source, sem, p, slot):
        return pltpu.make_async_remote_copy(
            source, rows_in.at[slot], sem, row_recv.at[slot],
            device_id={"ens": p * 2 + core}, device_id_type=MESH,
        )

    def col_copy(a, source, p, slot):
        return pltpu.make_async_remote_copy(
            source.at[of(a)], cols_in.at[slot, of(a)], col_send.at[a, p], col_recv.at[a, slot],
            device_id={"ens": p * 2 + core}, device_id_type=MESH,
        )

    tile_over = member(t, over[0], n)
    row_over = member(me, over[0], n)

    def send_tiles(a):
        for offset in near:
            p = member(t, offset, n)
            tile_copy(a, mine, tile_send.at[a, p], p, t).start()

        @pl.when(t != me)
        def _():
            col_copy(a, mine, t, me).start()

        @pl.when(t == me)
        def _():
            cols_in[me, of(a)] = mine[of(a)]

    def relay_tiles(a, offsets, on):
        for offset in offsets:
            p = member(t, offset, n)
            tile_copy(a, mine, tile_send.at[a, p], p, p).wait_recv()
            if on:
                tile_copy(a, tiles.at[p], tile_pass.at[a, p], tile_over, p).start()

            @pl.when(p != me)
            def _():
                col_copy(a, tiles.at[p], p, me).start()

            @pl.when(p == me)
            def _():
                cols_in[me, of(a)] = tiles[me, of(a)]

    send_tiles(0)
    for offset in near:
        p = member(me, offset, n)
        row_copy(mine, row_send.at[p], p, me).start()
    send_tiles(1)
    part[...] = jnp.zeros_like(part)

    counts_copy.wait()
    lane_ids = lax.broadcasted_iota(jnp.int32, (rows, WINDOW), 1)
    bead_ids = lax.broadcasted_iota(jnp.int32, (rows, WINDOW), 0)
    pick_row = lane_ids == bead_ids + row_off
    seg_row = jnp.sum(
        jnp.where(pick_row, seg_ref[:, pl.ds(row_start, WINDOW)].astype(F32), 0.0), axis=1, keepdims=True
    )
    seg_cols = jnp.broadcast_to(
        seg_ref[:, pl.ds(col_start, WINDOW)].astype(F32), (8, WINDOW)
    ).astype(jnp.bfloat16)
    counts_f = window[...].astype(F32).astype(jnp.bfloat16)
    pick_ids = lax.broadcasted_iota(jnp.int32, (LANES, WINDOW), 1)
    pick_bead = lax.broadcasted_iota(jnp.int32, (LANES, WINDOW), 0)
    for h in range(chunks):
        pick = (pick_ids == pick_bead + col_off + h * CHUNK) & (pick_bead < CHUNK)
        pick = pick.astype(F32).astype(jnp.bfloat16)
        count = against(counts_f, pick)
        same = seg_row == against(seg_cols, pick)[0:1, :]
        bead = lax.broadcasted_iota(jnp.int32, (rows, LANES), 1)
        diagonal = t * rows + lax.broadcasted_iota(jnp.int32, (rows, LANES), 0) == me * rows + h * CHUNK + bead
        weight = jnp.where(diagonal, 0.0, jnp.where(same, 1.0, 0.3))
        rest[h] = 0.5 - count / (count + 8.0)
        scale[h] = weight * (-1.0 / 64.0)

    relay_tiles(0, line, True)
    for offset in line:
        p = member(me, offset, n)
        row_copy(mine, row_send.at[p], p, p).wait_recv()
        row_copy(rows_in.at[p], row_pass.at[p], row_over, p).start()
    relay_tiles(0, over, False)
    relay_tiles(1, line, True)
    relay_tiles(1, over, False)

    def turn(block, target, h):
        block = block.reshape(lanes, LANES).T
        for c in range(3):
            at = pl.multiple_of(c * rows + h * CHUNK, 8)
            target[pl.ds(at, CHUNK), :] = block[c * CHUNK : (c + 1) * CHUNK, :]

    def norms(source, target, bias, h):
        x, y, z = (source[pl.ds(pl.multiple_of(c * rows + h * CHUNK, 8), CHUNK), :] for c in range(3))
        target[pl.ds(pl.multiple_of(h * CHUNK, 8), CHUNK), :] = bias - 0.5 * (x * x + y * y + z * z)

    lane = lax.broadcasted_iota(jnp.int32, (8, LANES), 1)

    def spread(ref, r):
        return jnp.broadcast_to(ref[pl.ds(r, 1), :], (8, lanes))

    def sigmoids(h):
        def col_block(b, carry):
            j = h * CHUNK + 8 * b
            at = [[spread(col_t, c * rows + j + q) for c in range(3)] for q in range(8)]
            bias = [spread(col_c, j + q) for q in range(8)]
            for k in range(blocks):
                own = slice(8 * k, 8 * k + 8)
                x, y, z = (row_t[c * rows + 8 * k : c * rows + 8 * k + 8, :] for c in range(3))
                ci = row_c[own, :]
                for q in range(8):
                    xj, yj, zj = at[q]
                    v = jnp.tanh(((bias[q] + ci) + xj * x) + (yj * y + zj * z))
                    tanhs[h * GROUP + b, k, q] = v
                    part[h, own, 8 * b + q : 8 * b + q + 1] = jnp.sum(v, axis=1, keepdims=True)
            return carry

        for b in range(GROUP):
            col_block(b, 0)

    def swap(h):
        return pltpu.make_async_remote_copy(
            part.at[h], other.at[h], core_send.at[h], core_recv.at[h],
            device_id={"ens": me * 2 + 1 - core}, device_id_type=MESH,
        )

    def weigh(h):
        mean = (part[h] + other[h]) * (0.5 / structs)
        weights[h] = scale[h] * (rest[h] + mean)

    def out_copy(g, p, slot):
        return pltpu.make_async_remote_copy(
            grad_s.at[g, p], parts_in.at[g, slot], out_send.at[g, p], out_recv.at[g, slot],
            device_id={"ens": p * 2 + core}, device_id_type=MESH,
        )

    def gather_pairs(g, acc, h):
        at = [pl.multiple_of(CHUNK * g + 8 * k, 8) for k in range(GROUP)]
        for b in range(GROUP):
            w = [weights[h, pl.ds(at[k], 8), :] for k in range(GROUP)]
            for q in range(8):
                j = h * CHUNK + 8 * b + q
                x, y, z = (spread(col_t, c * rows + j) for c in range(3))
                for k in range(GROUP):
                    v = tanhs[h * GROUP + b, GROUP * g + k, q]
                    wq = jnp.broadcast_to(w[k][:, 8 * b + q : 8 * b + q + 1], (8, lanes))
                    d = wq - wq * (v * v)
                    s, sx, sy, sz = acc[k]
                    acc[k] = [s + d, sx + d * x, sy + d * y, sz + d * z]
        return acc

    def row_group(g, wait=False):
        acc = [[jnp.zeros((8, lanes), F32)] * 4 for k in range(GROUP)]
        for h in range(chunks - 1):
            acc = gather_pairs(g, acc, h)

        if wait:
            swap(chunks - 1).wait()
            weigh(chunks - 1)

        acc = gather_pairs(g, acc, chunks - 1)
        for k in range(GROUP):
            for c in range(3):
                xi = row_t[pl.ds(pl.multiple_of(c * rows + CHUNK * g + 8 * k, 8), 8), :]
                grad_t[c * CHUNK + 8 * k : c * CHUNK + 8 * k + 8, :] = xi * acc[k][0] - acc[k][c + 1]
        grad_s[g] = grad_t[...].T.reshape(n, local_n, LANES)
        for offset in reversed(order):
            out_copy(g, member(me, offset, n), me).start()

    for offset in over:
        p = member(me, offset, n)
        row_copy(mine, row_send.at[p], p, p).wait_recv()
    for h in range(chunks):
        turn(rows_in[:, h], row_t, h)
        norms(row_t, row_c, 3.0, h)

    def first_pass(h, carry):
        turn(cols_in[:, h], col_t, h)
        norms(col_t, col_c, 0.0, h)
        sigmoids(h)
        swap(h).start()
        return carry

    for a, span in enumerate(parts):
        for offset in order:
            p = member(me, offset, n)
            col_copy(a, mine, p, p).wait_recv()
        lax.fori_loop(span[0], span[1], first_pass, 0)
    grad_t[3 * CHUNK :, :] = jnp.zeros((LANES - 3 * CHUNK, lanes), F32)
    for h in range(chunks - 1):
        swap(h).wait()
        weigh(h)
    row_group(0, True)

    @pl.loop(1, chunks)
    def _(g):
        row_group(g)


    def collect(g, carry):
        total = grad_s[g, me]
        for offset in order:
            p = member(me, offset, n)
            out_copy(g, p, p).wait_recv()
            total = total + parts_in[g, p]
        grad_s[g, me] = total
        return carry

    lax.fori_loop(0, chunks, collect, 0)
    for g in range(chunks):
        for c in range(3):
            out_ref[c, :, g * CHUNK : (g + 1) * CHUNK] = grad_s[g, me, :, c * CHUNK : (c + 1) * CHUNK]

    def drain(g, carry):
        for offset in order:
            p = member(me, offset, n)
            out_copy(g, p, p).wait_send()
        return carry

    lax.fori_loop(0, chunks, drain, 0)
    for offset in near:
        p, q = member(me, offset, n), member(t, offset, n)
        row_copy(mine, row_send.at[p], p, me).wait_send()
        for a in range(2):
            tile_copy(a, mine, tile_send.at[a, q], q, t).wait_send()
    for offset in line:
        p, q = member(me, offset, n), member(t, offset, n)
        row_copy(rows_in.at[p], row_pass.at[p], row_over, p).wait_send()
        for a in range(2):
            tile_copy(a, tiles.at[q], tile_pass.at[a, q], tile_over, q).wait_send()
    for offset in order:
        p = member(me, offset, n)
        for a in range(2):
            col_copy(a, mine, p, p).wait_send()


def solution(mesh):
    n = mesh.shape["tile"]

    def on_device(coords, counts, segments):
        local_n, _, rows = coords.shape
        structs = local_n * mesh.shape["ens"]
        lanes = n * local_n
        blocks = rows // 8
        chunks = rows // CHUNK
        vmem, dma = pltpu.VMEM, pltpu.SemaphoreType.DMA
        out = pl.pallas_call(
            functools.partial(kernel, n, structs),
            out_shape=jax.ShapeDtypeStruct((3, local_n, rows), F32),
            in_specs=[
                pl.BlockSpec(memory_space=pltpu.VMEM),
                pl.BlockSpec(memory_space=pl.ANY),
                pl.BlockSpec(memory_space=pltpu.VMEM),
            ],
            out_specs=pl.BlockSpec(memory_space=pltpu.VMEM),
            scratch_shapes=[
                vmem((chunks, local_n, LANES), F32),
                vmem((n, chunks, local_n, LANES), F32),
                vmem((n, chunks, local_n, LANES), F32),
                vmem((n, chunks, local_n, LANES), F32),
                vmem((3 * rows, lanes), F32),
                vmem((3 * rows, lanes), F32),
                vmem((rows, lanes), F32),
                vmem((rows, lanes), F32),
                vmem((blocks, blocks, 8, 8, lanes), F32),
                vmem((rows, WINDOW), jnp.int32),
                vmem((chunks, rows, LANES), F32),
                vmem((chunks, rows, LANES), F32),
                vmem((chunks, rows, LANES), F32),
                vmem((chunks, rows, LANES), F32),
                vmem((chunks, rows, LANES), F32),
                vmem((LANES, lanes), F32),
                vmem((chunks, n, local_n, LANES), F32),
                vmem((chunks, n, local_n, LANES), F32),
                dma((2, n)), dma((2, n)), dma((2, n)), dma((n,)), dma((n,)), dma((n,)), dma((2, n)), dma((2, n)),
                dma((chunks,)), dma((chunks,)), dma((chunks, n)), dma((chunks, n)), dma,
            ],
            compiler_params=pltpu.CompilerParams(
                collective_id=0, has_side_effects=True, vmem_limit_bytes=60 * 1024 * 1024
            ),
        )(coords.transpose(1, 0, 2), counts, segments.reshape(1, -1))
        return out.transpose(1, 0, 2)

    return jax.shard_map(
        on_device,
        mesh=mesh,
        in_specs=(P("ens", None, "tile"), P("tile", None), P()),
        out_specs=P("ens", None, "tile"),
        check_vma=False,
    )
```

time: 620 us -> 63.3 us (0.10); the launches traced: 610 us -> 63 us
  waiting for transfers between devices: 410 us -> 0 us
  blocking collectives: 78.5 us -> 0 us
  Pallas kernels: 0 us -> 60.3 us
  other arithmetic: 60.1 us -> 0 us
  matrix products: 27.9 us -> 0 us
  local copies, waits for them, and re-layouts: 18 us -> 2.67 us
  between operations: 14.1 us -> 0.01 us
    psum x1 -> x0, waiting for transfers between devices: 286 us -> none  [on_device(): pbar = lax.psum(total, 'ens') / structs]
    unnamed x3 -> x0, waiting for transfers between devices: 125 us -> none
    all_gather x1 -> x0, blocking collectives: 78.5 us -> none  [on_device(): all_coords = lax.all_gather(coords, 'tile', axis=2, tiled=True)]
    pallas_call x0 -> x1, Pallas kernels: none -> 60.3 us  [on_device(): pl.pallas_call(functools.partial(kernel, n, structs), out_shape=jax.Shape...]
    add x10 -> x0, other arithmetic: 31.3 us -> none  [the longest x8 29.8 us: accumulate(): return (total + pair_sigmoid(pair[0], pair[1]), None)]
    dot_general x16 -> x0, matrix products: 27.9 us -> none  [the longest x8 17.3 us: pair_terms(): jnp.einsum('cj,ij->ci', all_xyz, term, precision=lax.Precision.HIGHEST, p...]
    reduce_sum x24 -> x0, other arithmetic: 24.6 us -> none  [the longest x16 15.3 us: pair_sigmoid(): dist = jnp.sum(gap * gap, axis=0)]
    while x18 -> x0, local copies, waits for them, and re-layouts: 11.6 us -> none  [the longest x2 5.86 us: on_device(): own_parts, other_parts = lax.map(half_grads, (coords, all_coords))]
  transfers between devices with their start and end apart: 2 -> 0, of which waited for: 2 -> 0; matrix products, arithmetic and copies ran while one was open for 0% -> 0% of each run, Pallas kernels for 0% -> 0%
where the time goes in v2:
time: 63.3 us; the launch traced here: 63 us
  Pallas kernels  60.3 us (95%)
  local copies, waits for them, and re-layouts  2.67 us (4%)
    pallas_call x1, Pallas kernels, on_device(): pl.pallas_call(functools.partial(kernel, n, structs), out_shape=jax.Shape...  60.3 us
    unnamed x1, local copies, waits for them, and re-layouts  1.35 us
    reshape x1, local copies, waits for them, and re-layouts, on_device(): segments.reshape(1, -1)  1.33 us

profile of v2, /device:TPU:1, one launch (start us, length us, event | category | flops | bytes accessed | tf_op | source)
XLA Modules:
  0.0 63.0 jit_solution(8982047860074275551)
XLA Ops:
  0.0 1.3 %reshape.3.seg_ref = s32[1,3200]{1,0:T(1,128)} reshape(s32[3200]{0:T(1024)} %param.5) | data formatting | bytes 25600 | tf_op jit(solution)/shard_map/reshape | solution.py:373
  1.3 60.3 %shard_map.37 = f32[3,8,200]{2,1,0:T(8,128)} custom-call(f32[3,8,200]{2,1,0:T(8,128)} %bitcast.3, s32[200,3200]{1,0:T(8,128)} %counts_ref.1, s32[1,3200]{1,0:T(1,128)} %reshape.3.seg_ref), custom_call_target="tpu_custom_call" | custom-call | tf_op jit(solution)/shard_map/pallas_call | solution.py:339
  61.7 1.3 %copy.5 = f32[8,3,200]{2,0,1:T(8,128)} copy(f32[8,3,200]{2,0,1:T(8,128)} %bitcast.2) | data formatting | bytes 38400
